TPU v7x, 128 devices: a whole 4x4x4 slice. The times are simulated.
128 devices in a mesh: ctx: 32 (over z, y_lo, x), grp: 4 (over y_hi, core).
Axes of the slice: x: 4, y: 4 (y_hi: 2, y_lo: 2; y = y_hi * 2 + y_lo), z: 4, core: 2. Of those that a mesh axis runs over, the one named last changes fastest.
Arguments:
- query_input: bfloat16 [16384, 4096], P(('ctx', 'grp')), may hold values from -6 to 6
- key_input: bfloat16 [16384, 4096], P(('ctx', 'grp')), may hold values from -6 to 6
- value_input: bfloat16 [16384, 4096], P(('ctx', 'grp')), may hold values from -6 to 6
- out_grad: bfloat16 [16384, 4096], P(('ctx', 'grp')), may hold values from -6 to 6
- residues: float32 [8, 16], replicated, may hold values from -2 to 2
- decay_rates: float32 [8, 16], replicated, may hold values from 3.0517578e-06 to 0.15
Outputs:
- output: float32 [16384, 4096], P(('ctx', 'grp'))
- query_grad: float32 [16384, 4096], P(('ctx', 'grp'))
- key_grad: float32 [16384, 4096], P(('ctx', 'grp'))
- value_grad: float32 [16384, 4096], P(('ctx', 'grp'))
- residue_grad: float32 [8, 16], replicated
All inputs are finite; a program needn't handle non-finite values.
Results may differ from a plain program's by a relative error of at most 0.0055.
Values may be sent and summed in bfloat16 or wider, within the bound.
A program may use at most 192 MiB of HBM per device.

v0:
```python
import math
import jax
import jax.numpy as jnp
from jax import lax
from jax.sharding import PartitionSpec as P

GROUP = 512
HIGHEST = lax.Precision.HIGHEST


def entering(part, axis, combine, identity, reverse):
    count = lax.axis_size(axis)
    place = lax.axis_index(axis)
    ahead = count - 1 - place if reverse else place
    gathered = jax.tree.map(lambda a: lax.all_gather(a, axis), part)
    state = jax.tree.map(lambda a, e: jnp.zeros_like(a) + jnp.asarray(e, a.dtype), part, identity)

    def one(hop, state):
        source = count - 1 - hop if reverse else hop
        return combine(
            state, jax.tree.map(lambda a: lax.dynamic_index_in_dim(a, source, 0, False), gathered)
        )

    return lax.fori_loop(0, ahead, one, state)


def mode_tables(term_residues, decays, pairing, span):
    position = jnp.arange(span).astype(jnp.float32)
    distance = position[:, None] - position[None, :]
    causal_mask = distance >= 0.0
    lag_values = jnp.maximum(distance, 0.0)
    group_count = term_residues.shape[0]

    def one_mode(total, columns):
        res_column, decay_column = columns
        weight = jnp.where(
            causal_mask[None], jnp.exp(-decay_column[:, None, None] * lag_values[None]), 0.0
        )
        total = total + res_column[:, None, None] * weight
        return (total, jnp.sum(pairing * weight, axis=(1, 2)))

    start_total = jnp.zeros((group_count, span, span), jnp.float32)
    causal, inside = lax.scan(one_mode, start_total, (term_residues.T, decays.T))
    upper_part = causal.astype(jnp.bfloat16)
    lower_part = (causal - upper_part.astype(jnp.float32)).astype(jnp.bfloat16)
    return (upper_part, lower_part, inside.T)


def link_states(earlier, later):
    return (later[1][:, :, None] * earlier[0] + later[0], earlier[1] * later[1])


def convolve(product, inner_grad, term_residues, decays, carry_states):
    span, columns = product.shape
    group_count = columns // GROUP
    grouped = product.reshape(span, group_count, GROUP)
    grad_rows = inner_grad.reshape(span, group_count, GROUP)
    pairing = jnp.einsum("agc,bgc->gab", grad_rows, grouped, preferred_element_type=jnp.float32)
    upper_part, lower_part, inside = mode_tables(term_residues, decays, pairing, span)
    mixed_sum = jnp.einsum("gab,bgc->agc", upper_part, grouped, preferred_element_type=jnp.float32)
    mixed_sum = mixed_sum + jnp.einsum(
        "gab,bgc->agc", lower_part, grouped, preferred_element_type=jnp.float32
    )
    conv_sum = jnp.einsum("gab,agc->bgc", upper_part, grad_rows, preferred_element_type=jnp.float32)
    conv_sum = conv_sum + jnp.einsum(
        "gab,agc->bgc", lower_part, grad_rows, preferred_element_type=jnp.float32
    )
    position = jnp.arange(span).astype(jnp.float32)
    to_end = jnp.exp(-decays[:, :, None] * (span - 1.0 - position)[None, None, :])
    from_start = jnp.exp(-decays[:, :, None] * position[None, None, :])
    end_states = jnp.einsum("gmb,bgc->gmc", to_end, grouped.astype(jnp.float32), precision=HIGHEST)
    start_states = jnp.einsum(
        "gma,agc->gmc", from_start, grad_rows.astype(jnp.float32), precision=HIGHEST
    )
    factor = jnp.exp(-decays * float(span))
    carried_in, behind = carry_states(end_states, start_states, factor, span)
    rising = jnp.exp(-decays[:, :, None] * (position + 1.0)[None, None, :])
    falling = jnp.exp(-decays[:, :, None] * (span - position)[None, None, :])
    mixed_sum = mixed_sum + jnp.einsum(
        "gma,gmc->agc", term_residues[:, :, None] * rising, carried_in, precision=HIGHEST
    )
    conv_sum = conv_sum + jnp.einsum(
        "gmb,gmc->bgc", term_residues[:, :, None] * falling, behind, precision=HIGHEST
    )
    projected = jnp.einsum(
        "agc,gmc->gma", grad_rows.astype(jnp.float32), carried_in, precision=HIGHEST
    )
    residue_share = inside + jnp.sum(projected * rising, axis=2)
    return (mixed_sum.reshape(span, columns), conv_sum.reshape(span, columns), residue_share)


def finish(query_part, key_part, value_part, grad_part, mixed_out, conv_grad):
    output = query_part.astype(jnp.float32) * mixed_out
    query_grad = grad_part.astype(jnp.float32) * mixed_out
    key_grad = conv_grad * value_part.astype(jnp.float32)
    value_grad = conv_grad * key_part.astype(jnp.float32)
    return (output, query_grad, key_grad, value_grad)


def gated_inputs(query_input, key_input, value_input, out_grad):
    product = (key_input.astype(jnp.float32) * value_input.astype(jnp.float32)).astype(jnp.bfloat16)
    inner_grad = (out_grad.astype(jnp.float32) * query_input.astype(jnp.float32)).astype(
        jnp.bfloat16
    )
    return (product, inner_grad)


def channel_layout(query_input, key_input, value_input, out_grad, residues, decay_rates):
    product, inner_grad = gated_inputs(query_input, key_input, value_input, out_grad)
    prod_cols, grad_cols = (
        lax.all_to_all(product, "grp", split_axis=1, concat_axis=0, tiled=True),
        lax.all_to_all(inner_grad, "grp", split_axis=1, concat_axis=0, tiled=True),
    )
    row_count, columns = prod_cols.shape
    group_count = columns // GROUP
    first_group = lax.axis_index("grp") * group_count
    local_res = lax.dynamic_slice_in_dim(residues, first_group, group_count, 0)
    local_decay = lax.dynamic_slice_in_dim(decay_rates, first_group, group_count, 0)

    def carry_states(end_states, start_states, factor, span):
        neutral = (jnp.zeros_like(end_states), jnp.ones_like(factor))
        carried_in, spent_ahead = entering((end_states, factor), "ctx", link_states, neutral, False)
        behind, spent_behind = entering((start_states, factor), "ctx", link_states, neutral, True)
        return (carried_in, behind)

    mixed_cols, conv_cols, residue_share = convolve(
        prod_cols, grad_cols, local_res, local_decay, carry_states
    )
    mixed_rows, conv_rows = (
        lax.all_to_all(mixed_cols, "grp", split_axis=0, concat_axis=1, tiled=True),
        lax.all_to_all(conv_cols, "grp", split_axis=0, concat_axis=1, tiled=True),
    )
    results = finish(query_input, key_input, value_input, out_grad, mixed_rows, conv_rows)
    placed = lax.dynamic_update_slice_in_dim(
        jnp.zeros(residues.shape, jnp.float32), residue_share, first_group, 0
    )
    return (results, placed, row_count * lax.axis_size("ctx"))


def on_device(query_input, key_input, value_input, out_grad, residues, decay_rates):
    results, placed, length = channel_layout(
        query_input, key_input, value_input, out_grad, residues, decay_rates
    )
    summed = lax.psum(placed, ("ctx", "grp"))
    residue_grad = summed / (length * math.sqrt(GROUP))
    return (results[0], results[1], results[2], results[3], residue_grad)


def solution(mesh):
    in_specs = (
        P(("ctx", "grp"), None),
        P(("ctx", "grp"), None),
        P(("ctx", "grp"), None),
        P(("ctx", "grp"), None),
        P(),
        P(),
    )
    out_specs = (
        P(("ctx", "grp"), None),
        P(("ctx", "grp"), None),
        P(("ctx", "grp"), None),
        P(("ctx", "grp"), None),
        P(),
    )
    return jax.shard_map(
        on_device, mesh=mesh, in_specs=in_specs, out_specs=out_specs, check_vma=False
    )
```

profile of v0, /device:TPU:1, one launch (start us, length us, event | category | flops | bytes accessed | tf_op | source)
XLA Modules:
  0.0 491.0 jit_solution(2044057091201564266)
XLA Ops:
  7.2 1.8 fusion.5
  9.0 1.1 copy.101
  10.0 6.0 %all-to-all-start.1 = ((bf16[128,4,1024]{2,0,1:T(8,128)(2,1)}), bf16[128,4,1024]{2,0,1:T(8,128)(2,1)S(1)}, u32[]{:S(2)}, u32[]{:S(2)}) async-start(bf16[128,4,1024]{2,0,1:T(8,128)(2,1)} %bitcast.53), calls=%async_computation.1 | async-start | bytes 2097152 | tf_op jit(solution)/shard_map/all_to_all | solution.py:112
  16.9 14.2 %all-to-all-done.1 = bf16[128,4,1024]{2,0,1:T(8,128)(2,1)S(1)} async-done(((bf16[128,4,1024]{2,0,1:T(8,128)(2,1)}), bf16[128,4,1024]{2,0,1:T(8,128)(2,1)S(1)}, u32[]{:S(2)}, u32[]{:S(2)}) %all-to-all-start.1) | async-done | bytes 1048608 | tf_op jit(solution)/shard_map/all_to_all | solution.py:112
  31.1 1.0 copy-done.7
  32.1 1.8 reshape.76
  33.9 1.2 fusion.12
  35.4 1.1 copy.102
  36.5 5.1 %all-to-all-start = ((bf16[128,4,1024]{2,0,1:T(8,128)(2,1)}), bf16[128,4,1024]{2,0,1:T(8,128)(2,1)}, u32[]{:S(2)}, u32[]{:S(2)}) async-start(bf16[128,4,1024]{2,0,1:T(8,128)(2,1)} %bitcast.54), calls=%async_computation | async-start | bytes 2097152 | tf_op jit(solution)/shard_map/all_to_all | solution.py:111
  41.7 68.3 %all-gather.3 = f32[32,2,16]{2,1,0:T(2,128)S(1)} all-gather(f32[1,2,16]{2,1,0:T(2,128)S(1)} %get-tuple-element.293), channel_id=2, replica_groups=mesh['ctx'=32,'grp'=4] {'ctx'}, dimensions={0}, use_global_device_ids=true | all-gather | bytes 4224 | tf_op jit(solution)/shard_map/all_gather | solution.py:15
  110.1 2.6 reshape.75
  112.7 2.4 fusion.7
  115.1 3.3 fusion.9
  118.4 54.7 %while.43 = (s32[]{:T(128)}, f32[2,512,512]{2,1,0:T(8,128)S(1)}, f32[16,2]{1,0:T(8,128)S(1)}, f32[16,2]{1,0:T(8,128)S(1)}, f32[16,2]{1,0:T(8,128)S(1)}, /*index=...) while((s32[]{:T(128)}, f32[2,512,512]{2,1,0:T(8,128)S(1)}, ...), condition=%wide.region_2.3_spmd.clone.clone.clone, body=%wide.region_0.2_spmd.clone.clone.clone.sunk | while | flops 4718595 | bytes 8917183 | solution.py:43
  118.9 3.0 multiply_reduce_fusion.2
  122.3 3.0 multiply_reduce_fusion.2
  125.7 3.0 multiply_reduce_fusion.2
  129.1 3.0 multiply_reduce_fusion.2
  132.5 3.0 multiply_reduce_fusion.2
  135.9 3.0 multiply_reduce_fusion.2
  139.4 3.0 multiply_reduce_fusion.2
  142.8 3.0 multiply_reduce_fusion.2
  146.2 3.0 multiply_reduce_fusion.2
  149.6 3.0 multiply_reduce_fusion.2
  153.0 3.0 multiply_reduce_fusion.2
  156.4 3.0 multiply_reduce_fusion.2
  159.9 3.0 multiply_reduce_fusion.2
  163.3 3.0 multiply_reduce_fusion.2
  166.7 3.0 multiply_reduce_fusion.2
  170.1 3.0 multiply_reduce_fusion.2
  173.1 2.5 copy.78
  175.6 3.7 copy.71
  179.2 3.4 fusion.39
  182.6 2.0 fusion.43
  184.7 2.1 fusion.41
  186.7 2.1 fusion.44
  188.8 28.8 %while.42 = (s32[]{:T(128)}, f32[2,16,512]{2,1,0:T(8,128)S(1)}, s32[]{:T(128)}, f32[32,2,16]{2,1,0:T(2,128)S(1)}, f32[32,2,16,512]{3,2,1,0:T(8,128)}, /*index=5*/s32[]{:T(128)}, s32[]{:T(128)}, s32[]{:T(128)}, s32[]{:T(128)}) while((s32[]{:T(128)}, f32[2,16,512]{2,1,0:T(8,128)S(1)}, s32[]{:T(128)}, f32[32,2,16]{2,1,0:T(2,128)S(1)}, ...), condition=%wide.region_6.7_spmd, body=%wide.region_5.6_spmd.sunk | while | flops 32774 | bytes 197147 | solution.py:24
  188.9 0.9 bitcast_add_fusion.6
  189.8 0.9 bitcast_add_fusion.6
  190.7 0.9 bitcast_add_fusion.6
  191.7 0.9 bitcast_add_fusion.6
  192.6 0.9 bitcast_add_fusion.6
  193.5 0.9 bitcast_add_fusion.6
  194.4 0.9 bitcast_add_fusion.6
  195.4 0.9 bitcast_add_fusion.6
  199.1 0.9 bitcast_add_fusion.6
  200.0 0.9 bitcast_add_fusion.6
  200.9 0.9 bitcast_add_fusion.6
  208.3 0.9 bitcast_add_fusion.6
  214.8 0.9 bitcast_add_fusion.6
  217.6 5.5 %add_bitcast_fusion = f32[512,2,512]{0,2,1:T(8,128)} fusion(f32[2,512,512]{2,1,0:T(8,128)} %fusion.39, f32[2,512,512]{2,1,0:T(8,128)} %fusion.43, f32[2,16,512]{2,1,0:T(8,128)S(1)} %get-tuple-element.178, f32[512]{0:T(512)S(1)} %fusion.35, f32[2,16]{1,0:T(2,128)S(1)} %constant_dynamic-slice_fusion.1, f32[2,16]{1,0:T(2,128)S(1)} %get-tuple-element.294), kind=kOutput, calls=%fused_computation.21 | convolution fusion | flops 101744640 | bytes 6359296 | tf_op jit(solution)/shard_map/gmb,gmc->bgc/dot_general | solution.py:82
  223.1 1.9 all_to_all.62
  225.0 1.5 copy.81
  226.5 18.8 %all-to-all-start.3 = ((f32[4,128,1024]{1,2,0:T(8,128)}), f32[4,128,1024]{1,2,0:T(8,128)S(1)}, u32[]{:S(2)}, u32[]{:S(2)}) async-start(f32[4,128,1024]{1,2,0:T(8,128)} %copy.81), calls=%async_computation.3 | async-start | bytes 4194304 | tf_op jit(solution)/shard_map/all_to_all | solution.py:131
  245.3 77.5 %all-gather.7.cloned.1.call-done = f32[64,16,512]{2,1,0:T(8,128)} async-done(((f32[2,16,512]{2,1,0:T(8,128)}), f32[64,16,512]{2,1,0:T(8,128)}) %all-gather.7.cloned.1.call-update) | async-done | bytes 2097168 | tf_op jit(solution)/shard_map/all_gather | solution.py:15
  322.9 5.5 %add_bitcast_fusion.1 = f32[512,2,512]{0,2,1:T(8,128)} fusion(f32[2,512,512]{2,1,0:T(8,128)} %fusion.41, f32[2,512,512]{2,1,0:T(8,128)} %fusion.44, f32[2,16,512]{2,1,0:T(8,128)S(1)} %get-tuple-element.177, f32[512]{0:T(512)S(1)} %fusion.33, f32[2,16]{1,0:T(2,128)S(1)} %constant_dynamic-slice_fusion.1, f32[2,16]{1,0:T(2,128)S(1)} %get-tuple-element.294), kind=kOutput, calls=%fused_computation.22 | convolution fusion | flops 101744640 | bytes 6359296 | tf_op jit(solution)/shard_map/gma,gmc->agc/dot_general | solution.py:79
  328.4 2.9 all_to_all.58
  331.2 3.0 copy.75
  334.3 26.2 %all-to-all-start.2 = ((f32[4,128,1024]{1,2,0:T(8,128)}), f32[4,128,1024]{1,2,0:T(8,128)}, u32[]{:S(2)}, u32[]{:S(2)}) async-start(f32[4,128,1024]{1,2,0:T(8,128)} %copy.75), calls=%async_computation.2 | async-start | bytes 4194304 | tf_op jit(solution)/shard_map/all_to_all | solution.py:130
  360.6 1.0 fusion.6
  361.6 110.7 %psum.7 = f32[8,16]{1,0:T(8,128)S(1)} all-reduce(f32[8,16]{1,0:T(8,128)S(1)} %fusion.36), channel_id=1, replica_groups=mesh['ctx'=32,'grp'=4] {'ctx','grp'}, use_global_device_ids=true, to_apply=%region_8.9 | all-reduce | flops 128 | bytes 1024 | tf_op jit(solution)/shard_map/psum | solution.py:144
  472.9 1.8 copy.82
  474.8 3.0 copy.76
  477.8 6.3 %convert_multiply_fusion = (f32[128,4096]{1,0:T(8,128)}, f32[128,4096]{1,0:T(8,128)}, f32[128,4096]{1,0:T(8,128)}, f32[128,4096]{1,0:T(8,128)}) fusion(f32[128,4096]{1,0:T(8,128)} %copy.76, bf16[128,4096]{1,0:T(8,128)(2,1)} %param.15, bf16[128,4096]{1,0:T(8,128)(2,1)} %param.12, f32[128,4096]{1,0:T(8,128)S(1)} %copy-done.3, ...), kind=kLoop, calls=%fused_computation.13 | loop fusion | flops 4194304 | bytes 16777216 | tf_op jit(solution)/shard_map/mul | solution.py:94
  (154 shorter events, 25.5 us)
Async XLA Ops:
  7.2 34.5 %copy-start = (f32[8,16]{1,0:T(8,128)S(1)}, f32[8,16]{1,0:T(8,128)}, u32[]{:S(2)}) copy-start(f32[8,16]{1,0:T(8,128)} %param.16) | copy-start | bytes 1540
  10.0 21.1 %all-to-all-start.1 = ((bf16[128,4,1024]{2,0,1:T(8,128)(2,1)}), bf16[128,4,1024]{2,0,1:T(8,128)(2,1)S(1)}, u32[]{:S(2)}, u32[]{:S(2)}) async-start(bf16[128,4,1024]{2,0,1:T(8,128)(2,1)} %bitcast.53), calls=%async_computation.1 | async-start | bytes 2097152 | tf_op jit(solution)/shard_map/all_to_all | solution.py:112
  16.0 19.1 %copy-start.4 = (bf16[128,4096]{1,0:T(8,128)(2,1)S(1)}, bf16[128,4096]{1,0:T(8,128)(2,1)}, u32[]{:S(2)}) copy-start(bf16[128,4096]{1,0:T(8,128)(2,1)} %param.14) | copy-start | bytes 3145732
  16.0 19.2 %copy-start.6 = (bf16[128,4096]{1,0:T(8,128)(2,1)S(1)}, bf16[128,4096]{1,0:T(8,128)(2,1)}, u32[]{:S(2)}) copy-start(bf16[128,4096]{1,0:T(8,128)(2,1)} %param.13) | copy-start | bytes 3145732
  16.0 172.8 %all-gather.9.cloned.1.call-start = ((), (), s32[]{:S(2)}) async-start(), calls=%async_computation.5 | async-start | bytes 2162688 | tf_op jit(solution)/shard_map/all_gather | solution.py:15
  31.1 1.0 copy-start.7
  36.5 73.6 %all-to-all-start = ((bf16[128,4,1024]{2,0,1:T(8,128)(2,1)}), bf16[128,4,1024]{2,0,1:T(8,128)(2,1)}, u32[]{:S(2)}, u32[]{:S(2)}) async-start(bf16[128,4,1024]{2,0,1:T(8,128)(2,1)} %bitcast.54), calls=%async_computation | async-start | bytes 2097152 | tf_op jit(solution)/shard_map/all_to_all | solution.py:111
  41.6 281.3 %all-gather.7.cloned.1.call-start = ((), (), s32[]{:S(2)}) async-start(), calls=%async_computation.4 | async-start | bytes 2162688 | tf_op jit(solution)/shard_map/all_gather | solution.py:15
  179.2 3.4 copy-start.2
  182.6 2.1 copy-start.1
  226.5 107.8 %all-to-all-start.3 = ((f32[4,128,1024]{1,2,0:T(8,128)}), f32[4,128,1024]{1,2,0:T(8,128)S(1)}, u32[]{:S(2)}, u32[]{:S(2)}) async-start(f32[4,128,1024]{1,2,0:T(8,128)} %copy.81), calls=%async_computation.3 | async-start | bytes 4194304 | tf_op jit(solution)/shard_map/all_to_all | solution.py:131
  334.3 140.5 %all-to-all-start.2 = ((f32[4,128,1024]{1,2,0:T(8,128)}), f32[4,128,1024]{1,2,0:T(8,128)}, u32[]{:S(2)}, u32[]{:S(2)}) async-start(f32[4,128,1024]{1,2,0:T(8,128)} %copy.75), calls=%async_computation.2 | async-start | bytes 4194304 | tf_op jit(solution)/shard_map/all_to_all | solution.py:130
  474.8 3.0 copy-start.3
  474.8 3.0 copy-start.5
Sparse Core Ops, SparseCore 0:
  35.3 132.3 all-gather.8
  169.3 153.5 all-gather.6
where the time goes:
time: 494 us; the launch traced here: 491 us
  blocking collectives  179 us (36%)
  other arithmetic  91.8 us (19%)
  waiting for transfers between devices  91.8 us (19%)
  starting transfers between devices  56.1 us (11%)
  local copies, waits for them, and re-layouts  28.8 us (6%)
  matrix products  28.5 us (6%)
  between operations  14.1 us (3%)
    psum x1, blocking collectives, on_device(): summed = lax.psum(placed, ('ctx', 'grp'))  111 us
    all_gather x2, waiting for transfers between devices, entering(): gathered = jax.tree.map(lambda a: lax.all_gather(a, axis), part)  77.6 us
    all_gather x1, blocking collectives, entering(): gathered = jax.tree.map(lambda a: lax.all_gather(a, axis), part)  68.3 us
    reduce_sum x16, other arithmetic, one_mode(): return (total, jnp.sum(pairing * weight, axis=(1, 2)))  47.3 us
    add x31, other arithmetic, link_states(): return (later[1][:, :, None] * earlier[0] + later[0], earlier[1] * later[1])  28.6 us
    all_to_all x1, starting transfers between devices, channel_layout(): lax.all_to_all(mixed_cols, 'grp', split_axis=0, concat_axis=1, tiled=True)  26.2 us
    all_to_all x1, starting transfers between devices, channel_layout(): lax.all_to_all(conv_cols, 'grp', split_axis=0, concat_axis=1, tiled=True)  18.8 us
    all_to_all x1, waiting for transfers between devices, channel_layout(): lax.all_to_all(inner_grad, 'grp', split_axis=1, concat_axis=0, tiled=True)  14.2 us
  transfers between devices with their start and end apart: 6, of which 2 were waited for; matrix products, arithmetic and copies ran while one was open for 26% of the time, Pallas kernels for 0%

commit v1 on v0

--- a/solution.py
+++ b/solution.py
@@ -141,7 +141,7 @@
     results, placed, length = channel_layout(
         query_input, key_input, value_input, out_grad, residues, decay_rates
     )
-    summed = lax.psum(placed, ("ctx", "grp"))
+    summed = jnp.sum(lax.all_gather(placed, ("ctx", "grp")), axis=0)
     residue_grad = summed / (length * math.sqrt(GROUP))
     return (results[0], results[1], results[2], results[3], residue_grad)
 

time: 494 us -> 605 us (1.22)
  blocking collectives: 179 us -> 290 us
    all_gather x0 -> x1, blocking collectives: none -> 222 us  [on_device(): summed = jnp.sum(lax.all_gather(placed, ('ctx', 'grp')), axis=0)]
    psum x1 -> x0, blocking collectives: 111 us -> none  [on_device(): summed = lax.psum(placed, ('ctx', 'grp'))]
  transfers between devices with their start and end apart: 6 -> 6, of which waited for: 2 -> 2; matrix products, arithmetic and copies ran while one was open for 26% -> 21% of each run, Pallas kernels for 0% -> 0%
where the time goes in v1:
time: 605 us; the launch traced here: 602 us
  blocking collectives  290 us (48%)
  other arithmetic  92 us (15%)
  waiting for transfers between devices  91.8 us (15%)
  starting transfers between devices  56.1 us (9%)
  local copies, waits for them, and re-layouts  28.8 us (5%)
  matrix products  28.5 us (5%)
  between operations  14.1 us (2%)
    all_gather x1, blocking collectives, on_device(): summed = jnp.sum(lax.all_gather(placed, ('ctx', 'grp')), axis=0)  222 us
    all_gather x2, waiting for transfers between devices, entering(): gathered = jax.tree.map(lambda a: lax.all_gather(a, axis), part)  77.6 us
    all_gather x1, blocking collectives, entering(): gathered = jax.tree.map(lambda a: lax.all_gather(a, axis), part)  68.3 us
    reduce_sum x16, other arithmetic, one_mode(): return (total, jnp.sum(pairing * weight, axis=(1, 2)))  47.3 us
    add x31, other arithmetic, link_states(): return (later[1][:, :, None] * earlier[0] + later[0], earlier[1] * later[1])  28.6 us
    all_to_all x1, starting transfers between devices, channel_layout(): lax.all_to_all(mixed_cols, 'grp', split_axis=0, concat_axis=1, tiled=True)  26.2 us
    all_to_all x1, starting transfers between devices, channel_layout(): lax.all_to_all(conv_cols, 'grp', split_axis=0, concat_axis=1, tiled=True)  18.8 us
    all_to_all x1, waiting for transfers between devices, channel_layout(): lax.all_to_all(inner_grad, 'grp', split_axis=1, concat_axis=0, tiled=True)  14.2 us
  transfers between devices with their start and end apart: 6, of which 2 were waited for; matrix products, arithmetic and copies ran while one was open for 21% of the time, Pallas kernels for 0%

profile of v1, /device:TPU:1, one launch (start us, length us, event | category | flops | bytes accessed | tf_op | source)
XLA Modules:
  0.0 602.2 jit_solution(5596245123580601130)
XLA Ops:
  7.2 1.8 fusion.5
  9.0 1.1 copy.101
  10.0 6.0 all-to-all-start.1
  16.9 14.2 %all-to-all-done.1 = bf16[128,4,1024]{2,0,1:T(8,128)(2,1)S(1)} async-done(((bf16[128,4,1024]{2,0,1:T(8,128)(2,1)}), bf16[128,4,1024]{2,0,1:T(8,128)(2,1)S(1)}, u32[]{:S(2)}, u32[]{:S(2)}) %all-to-all-start.1) | async-done | bytes 1048608 | tf_op jit(solution)/shard_map/all_to_all | solution.py:112
  31.1 1.0 copy-done.7
  32.1 1.8 reshape.78
  33.9 1.2 fusion.12
  35.4 1.1 copy.102
  36.5 5.1 all-to-all-start
  41.7 68.3 %all-gather.3 = f32[32,2,16]{2,1,0:T(2,128)S(1)} all-gather(f32[1,2,16]{2,1,0:T(2,128)S(1)} %get-tuple-element.293), channel_id=2, replica_groups=mesh['ctx'=32,'grp'=4] {'ctx'}, dimensions={0}, use_global_device_ids=true | all-gather | bytes 4224 | tf_op jit(solution)/shard_map/all_gather | solution.py:15
  110.1 2.6 reshape.77
  112.7 2.4 fusion.7
  115.1 3.3 fusion.9
  118.4 54.7 %while.43 = (s32[]{:T(128)}, f32[2,512,512]{2,1,0:T(8,128)S(1)}, f32[16,2]{1,0:T(8,128)S(1)}, f32[16,2]{1,0:T(8,128)S(1)}, f32[16,2]{1,0:T(8,128)S(1)}, /*index=...) while((s32[]{:T(128)}, f32[2,512,512]{2,1,0:T(8,128)S(1)}, ...), condition=%wide.region_2.3_spmd.clone.clone.clone, body=%wide.region_0.2_spmd.clone.clone.clone.sunk | while | flops 4718595 | bytes 8917183 | solution.py:43
  118.9 3.0 multiply_reduce_fusion.2
  122.3 3.0 multiply_reduce_fusion.2
  125.7 3.0 multiply_reduce_fusion.2
  129.1 3.0 multiply_reduce_fusion.2
  132.5 3.0 multiply_reduce_fusion.2
  135.9 3.0 multiply_reduce_fusion.2
  139.4 3.0 multiply_reduce_fusion.2
  142.8 3.0 multiply_reduce_fusion.2
  146.2 3.0 multiply_reduce_fusion.2
  149.6 3.0 multiply_reduce_fusion.2
  153.0 3.0 multiply_reduce_fusion.2
  156.4 3.0 multiply_reduce_fusion.2
  159.9 3.0 multiply_reduce_fusion.2
  163.3 3.0 multiply_reduce_fusion.2
  166.7 3.0 multiply_reduce_fusion.2
  170.1 3.0 multiply_reduce_fusion.2
  173.1 2.5 copy.78
  175.6 3.7 copy.71
  179.2 3.4 fusion.38
  182.6 2.0 fusion.42
  184.7 2.1 fusion.40
  186.7 2.1 fusion.43
  188.8 28.8 %while.42 = (s32[]{:T(128)}, f32[2,16,512]{2,1,0:T(8,128)S(1)}, s32[]{:T(128)}, f32[32,2,16]{2,1,0:T(2,128)S(1)}, f32[32,2,16,512]{3,2,1,0:T(8,128)}, /*index=5*/s32[]{:T(128)}, s32[]{:T(128)}, s32[]{:T(128)}, s32[]{:T(128)}) while((s32[]{:T(128)}, f32[2,16,512]{2,1,0:T(8,128)S(1)}, s32[]{:T(128)}, f32[32,2,16]{2,1,0:T(2,128)S(1)}, ...), condition=%wide.region_6.7_spmd, body=%wide.region_5.6_spmd.sunk | while | flops 32774 | bytes 197147 | solution.py:24
  188.9 0.9 bitcast_add_fusion.6
  189.8 0.9 bitcast_add_fusion.6
  190.7 0.9 bitcast_add_fusion.6
  191.7 0.9 bitcast_add_fusion.6
  192.6 0.9 bitcast_add_fusion.6
  193.5 0.9 bitcast_add_fusion.6
  194.4 0.9 bitcast_add_fusion.6
  195.4 0.9 bitcast_add_fusion.6
  199.1 0.9 bitcast_add_fusion.6
  200.0 0.9 bitcast_add_fusion.6
  200.9 0.9 bitcast_add_fusion.6
  208.3 0.9 bitcast_add_fusion.6
  214.8 0.9 bitcast_add_fusion.6
  217.6 5.5 add_bitcast_fusion
  223.1 1.9 all_to_all.62
  225.0 1.5 copy.81
  226.5 18.8 %all-to-all-start.3 = ((f32[4,128,1024]{1,2,0:T(8,128)}), f32[4,128,1024]{1,2,0:T(8,128)S(1)}, u32[]{:S(2)}, u32[]{:S(2)}) async-start(f32[4,128,1024]{1,2,0:T(8,128)} %copy.81), calls=%async_computation.3 | async-start | bytes 4194304 | tf_op jit(solution)/shard_map/all_to_all | solution.py:131
  245.3 77.5 %all-gather.7.cloned.1.call-done = f32[64,16,512]{2,1,0:T(8,128)} async-done(((f32[2,16,512]{2,1,0:T(8,128)}), f32[64,16,512]{2,1,0:T(8,128)}) %all-gather.7.cloned.1.call-update) | async-done | bytes 2097168 | tf_op jit(solution)/shard_map/all_gather | solution.py:15
  322.9 5.5 add_bitcast_fusion.1
  328.4 2.9 all_to_all.58
  331.2 3.0 copy.75
  334.3 26.2 %all-to-all-start.2 = ((f32[4,128,1024]{1,2,0:T(8,128)}), f32[4,128,1024]{1,2,0:T(8,128)}, u32[]{:S(2)}, u32[]{:S(2)}) async-start(f32[4,128,1024]{1,2,0:T(8,128)} %copy.75), calls=%async_computation.2 | async-start | bytes 4194304 | tf_op jit(solution)/shard_map/all_to_all | solution.py:130
  360.6 1.0 fusion.6
  361.6 221.9 %all_gather.33 = f32[128,8,16]{2,1,0:T(8,128)S(1)} all-gather(f32[1,8,16]{2,1,0:T(8,128)S(1)} %bitcast_dynamic-update-slice_fusion), channel_id=1, replica_groups=mesh['ctx'=32,'grp'=4] {'ctx','grp'}, dimensions={0}, use_global_device_ids=true | all-gather | bytes 66048 | tf_op jit(solution)/shard_map/all_gather | solution.py:144
  584.2 1.8 copy.82
  586.0 3.0 copy.76
  589.1 6.3 %convert_multiply_fusion = (f32[128,4096]{1,0:T(8,128)}, f32[128,4096]{1,0:T(8,128)}, f32[128,4096]{1,0:T(8,128)}, f32[128,4096]{1,0:T(8,128)}) fusion(f32[128,4096]{1,0:T(8,128)} %copy.76, bf16[128,4096]{1,0:T(8,128)(2,1)} %param.15, bf16[128,4096]{1,0:T(8,128)(2,1)} %param.12, f32[128,4096]{1,0:T(8,128)S(1)} %copy-done.3, ...), kind=kLoop, calls=%fused_computation.13 | loop fusion | flops 4194304 | bytes 16777216 | tf_op jit(solution)/shard_map/mul | solution.py:94
  (155 shorter events, 25.6 us)
Async XLA Ops:
  7.2 34.5 %copy-start = (f32[8,16]{1,0:T(8,128)S(1)}, f32[8,16]{1,0:T(8,128)}, u32[]{:S(2)}) copy-start(f32[8,16]{1,0:T(8,128)} %param.16) | copy-start | bytes 1540
  10.0 21.1 %all-to-all-start.1 = ((bf16[128,4,1024]{2,0,1:T(8,128)(2,1)}), bf16[128,4,1024]{2,0,1:T(8,128)(2,1)S(1)}, u32[]{:S(2)}, u32[]{:S(2)}) async-start(bf16[128,4,1024]{2,0,1:T(8,128)(2,1)} %bitcast.55), calls=%async_computation.1 | async-start | bytes 2097152 | tf_op jit(solution)/shard_map/all_to_all | solution.py:112
  16.0 19.1 %copy-start.4 = (bf16[128,4096]{1,0:T(8,128)(2,1)S(1)}, bf16[128,4096]{1,0:T(8,128)(2,1)}, u32[]{:S(2)}) copy-start(bf16[128,4096]{1,0:T(8,128)(2,1)} %param.14) | copy-start | bytes 3145732
  16.0 19.2 %copy-start.6 = (bf16[128,4096]{1,0:T(8,128)(2,1)S(1)}, bf16[128,4096]{1,0:T(8,128)(2,1)}, u32[]{:S(2)}) copy-start(bf16[128,4096]{1,0:T(8,128)(2,1)} %param.13) | copy-start | bytes 3145732
  16.0 172.8 %all-gather.9.cloned.1.call-start = ((), (), s32[]{:S(2)}) async-start(), calls=%async_computation.5 | async-start | bytes 2162688 | tf_op jit(solution)/shard_map/all_gather | solution.py:15
  31.1 1.0 copy-start.7
  36.5 73.6 %all-to-all-start = ((bf16[128,4,1024]{2,0,1:T(8,128)(2,1)}), bf16[128,4,1024]{2,0,1:T(8,128)(2,1)}, u32[]{:S(2)}, u32[]{:S(2)}) async-start(bf16[128,4,1024]{2,0,1:T(8,128)(2,1)} %bitcast.56), calls=%async_computation | async-start | bytes 2097152 | tf_op jit(solution)/shard_map/all_to_all | solution.py:111
  41.6 281.3 %all-gather.7.cloned.1.call-start = ((), (), s32[]{:S(2)}) async-start(), calls=%async_computation.4 | async-start | bytes 2162688 | tf_op jit(solution)/shard_map/all_gather | solution.py:15
  179.2 3.4 copy-start.2
  182.6 2.1 copy-start.1
  226.5 107.8 %all-to-all-start.3 = ((f32[4,128,1024]{1,2,0:T(8,128)}), f32[4,128,1024]{1,2,0:T(8,128)S(1)}, u32[]{:S(2)}, u32[]{:S(2)}) async-start(f32[4,128,1024]{1,2,0:T(8,128)} %copy.81), calls=%async_computation.3 | async-start | bytes 4194304 | tf_op jit(solution)/shard_map/all_to_all | solution.py:131
  334.3 251.7 %all-to-all-start.2 = ((f32[4,128,1024]{1,2,0:T(8,128)}), f32[4,128,1024]{1,2,0:T(8,128)}, u32[]{:S(2)}, u32[]{:S(2)}) async-start(f32[4,128,1024]{1,2,0:T(8,128)} %copy.75), calls=%async_computation.2 | async-start | bytes 4194304 | tf_op jit(solution)/shard_map/all_to_all | solution.py:130
  586.0 3.0 copy-start.3
  586.0 3.0 copy-start.5
Sparse Core Ops, SparseCore 0:
  35.3 132.3 all-gather.8
  169.3 153.5 all-gather.6
